TPU v7x, 32 devices: a whole 2x2x4 slice. The times are simulated.
32 devices in a mesh: gx: 8 (over z, y), gy: 4 (over x, core).
Axes of the slice: x: 2, y: 2, z: 4, core: 2. Of those that a mesh axis runs over, the one named last changes fastest.
Arguments:
- point_feats: bfloat16 [32, 262144], P(None, ('gx', 'gy')), may hold values from -1 to 1
- point_targets: bfloat16 [262144], P(('gx', 'gy')), may hold values from -6 to 6
- point_lists: int32 [32768, 8], P(('gx', 'gy')), may hold values from -1 to 8191, as said below
- brick_adjacency: int32 [1024, 4], P(('gx', 'gy')), may hold values from -1 to 1023, as said below
- voxel_feats: float32 [1024, 32, 512], P(('gx', 'gy')), may hold values from -0.25 to 0.25
- voxel_reg: float32 [1024, 512], P(('gx', 'gy')), may hold values from 0.25 to 2
Outputs:
- solution: float32 [1024, 512], P(('gx', 'gy'))
- residual: float32 [1024, 512], P(('gx', 'gy'))
Inputs may be any that keep to these rules, and one draw needn't show every extreme that they name: `point_lists`: row s * 1024 + b lists, in its first slots, distinct indices of the points of source device s in brick b, all within that device's rows b * 8 to b * 8 + 7, then -1 in the remaining slots. Point rows named by no list are unused. `brick_adjacency`: entry k of brick b is the lattice neighbour of b in direction k (minus along the road, plus along the road, minus across, plus across) or -1; the relation is symmetric and -1 wherever the neighbour lies outside the lattice.
All inputs are finite; a program needn't handle non-finite values.
Results may differ from a plain program's by a relative error of at most 0.0003.
Values may be sent and summed in bfloat16 or wider, within the bound.
A program may use at most 64 MiB of HBM per device.

v0:
```python
import jax
import jax.numpy as jnp
from jax import lax
from jax.sharding import PartitionSpec as P

BX = 8
BY = 4
ITERS = 3
coupling_weight = 1.0


def extended(block, sides, width):
    for axis, dim in sides:
        count = lax.axis_size(axis)
        forward = [(i, i + 1) for i in range(count - 1)]
        backward = [(target, source) for source, target in forward]
        low = lax.ppermute(
            lax.slice_in_dim(block, block.shape[dim] - width, None, axis=dim), axis, forward
        )
        high = lax.ppermute(lax.slice_in_dim(block, 0, width, axis=dim), axis, backward)
        block = jnp.concatenate([low, block, high], axis=dim)
    return block


def neighbour_sum(padded, mask):
    total = mask[..., 0:1] * padded[:-2, 1:-1] + mask[..., 1:2] * padded[2:, 1:-1]
    return total + mask[..., 2:3] * padded[1:-1, :-2] + mask[..., 3:4] * padded[1:-1, 2:]


def shards(point_feats, point_targets, point_lists, brick_adjacency, voxel_feats, voxel_reg):
    feat_count = point_feats.shape[0]
    brick_total, slots = point_lists.shape
    local_bricks = voxel_feats.shape[0]
    devices = brick_total // local_bricks
    live = point_lists >= 0
    offset = point_lists - jnp.arange(brick_total, dtype=jnp.int32)[:, None] * slots
    choose = (offset[:, :, None] == jnp.arange(slots, dtype=jnp.int32)[None, None, :]) & live[
        :, :, None
    ]
    choose = choose.astype(jnp.bfloat16)
    blocks = point_feats.reshape(feat_count, brick_total, slots)
    picked = jnp.einsum("ibd,bcd->ibc", blocks, choose, preferred_element_type=jnp.float32).astype(
        jnp.bfloat16
    )
    target_blocks = point_targets.reshape(brick_total, slots)
    targets = jnp.einsum(
        "bd,bcd->bc", target_blocks, choose, preferred_element_type=jnp.float32
    ).astype(jnp.bfloat16)
    sending = picked.reshape(feat_count, devices, local_bricks * slots)
    target_rows = targets.reshape(1, devices, local_bricks * slots)
    got_feats, got_targets = (
        lax.all_to_all(sending, ("gx", "gy"), split_axis=1, concat_axis=1, tiled=True),
        lax.all_to_all(target_rows, ("gx", "gy"), split_axis=1, concat_axis=1, tiled=True),
    )
    got_feats = got_feats.reshape(feat_count, devices, local_bricks, slots)
    got_targets = got_targets.reshape(devices, local_bricks, slots)
    moments = jnp.einsum("isbc,jsbc->bij", got_feats, got_feats, preferred_element_type=jnp.float32)
    gathered = jnp.einsum(
        "sbc,isbc->bi", got_targets, got_feats, preferred_element_type=jnp.float32
    )
    mask = (brick_adjacency >= 0).astype(jnp.float32).reshape(BX, BY, 4)
    degree = jnp.sum(mask, axis=-1, keepdims=True)

    def operate(vector):
        projected = jnp.einsum("bik,bk->bi", voxel_feats, vector, precision=lax.Precision.HIGHEST)
        lattice = projected.reshape(BX, BY, feat_count)
        padded = extended(lattice, (("gx", 0), ("gy", 1)), 1)
        coupled = (degree * lattice - neighbour_sum(padded, mask)).reshape(local_bricks, feat_count)
        middle = jnp.einsum("bij,bj->bi", moments, projected, precision=lax.Precision.HIGHEST)
        middle = middle + coupling_weight * coupled
        back = jnp.einsum("bik,bi->bk", voxel_feats, middle, precision=lax.Precision.HIGHEST)
        return back + voxel_reg * vector

    def two_products(values, image):
        return lax.psum((jnp.sum(values * values), jnp.sum(values * image)), ("gx", "gy"))

    rhs = jnp.einsum("bik,bi->bk", voxel_feats, gathered, precision=lax.Precision.HIGHEST)
    solution = jnp.zeros_like(rhs)
    residual = rhs
    image = operate(residual)
    norm_now, product = two_products(residual, image)
    alpha = norm_now / product
    direction, carried = (residual, image)
    for iteration in range(ITERS):
        solution = solution + alpha * direction
        residual = residual - alpha * carried
        if iteration + 1 < ITERS:
            image = operate(residual)
            norm_next, product = two_products(residual, image)
            ratio = norm_next / norm_now
            alpha = norm_next / (product - ratio * norm_next / alpha)
            direction = residual + ratio * direction
            carried = image + ratio * carried
            norm_now = norm_next
    return (solution, residual)


def solution(mesh):
    placed = (
        P(None, ("gx", "gy")),
        P(("gx", "gy")),
        P(("gx", "gy"), None),
        P(("gx", "gy"), None),
        P(("gx", "gy"), None, None),
        P(("gx", "gy"), None),
    )
    return jax.shard_map(
        shards,
        mesh=mesh,
        in_specs=placed,
        out_specs=(P(("gx", "gy"), None), P(("gx", "gy"), None)),
        check_vma=False,
    )
```

profile of v0, /device:TPU:0, one launch (start us, length us, event | category | flops | bytes accessed | tf_op | source)
XLA Modules:
  0.0 251.1 jit_solution(11795975120160489143)
XLA Ops:
  2.8 2.1 reshape.98
  4.9 5.8 %fusion.3 = f32[1024,1,8]{2,1,0:T(1,128)S(1)} fusion(bf16[1024,8,1]{1,2,0:T(2,128)(2,1)} %reshape.98, s32[1024,8]{1,0:T(8,128)S(1)} %copy.33, pred[1024,8]{1,0:T(8,128)(4,1)S(1)} %copy.34), kind=kOutput, calls=%fused_computation.3 | convolution fusion | flops 262144 | bytes 90112 | tf_op jit(solution)/shard_map/bd,bcd->bc/dot_general | solution.py:46
  12.9 7.3 %all-to-all-start = ((bf16[32,2,128]{2,1,0:T(2,128)(2,1)}), bf16[32,2,128]{2,1,0:T(2,128)(2,1)S(1)}, u32[]{:S(2)}, u32[]{:S(2)}) async-start(bf16[32,2,128]{2,1,0:T(2,128)(2,1)} %reshape.100), calls=%async_computation | async-start | bytes 32768 | tf_op jit(solution)/shard_map/all_to_all | solution.py:53
  20.3 1.8 copy.37
  22.1 7.1 %fusion.10 = bf16[1024,8,32]{2,1,0:T(8,128)(2,1)} fusion(bf16[32,8192]{0,1:T(8,128)(2,1)} %copy.37, s32[1024,8]{1,0:T(8,128)S(1)} %copy.33, pred[1024,8]{1,0:T(8,128)(4,1)S(1)} %copy-done.5), kind=kOutput, calls=%fused_computation.9 | convolution fusion | flops 4587520 | bytes 1089536 | tf_op jit(solution)/shard_map/ibd,bcd->ibc/dot_general | solution.py:42
  29.2 2.6 %copy.38 = bf16[32,32,256]{2,0,1:T(8,128)(2,1)} copy(bf16[32,32,256]{0,2,1:T(8,128)(2,1)} %bitcast.158) | data formatting | bytes 1048576 | tf_op jit(solution)/shard_map/reshape | solution.py:49
  31.8 5.8 %all-to-all-start.1 = ((bf16[32,32,256]{2,0,1:T(8,128)(2,1)}), bf16[32,32,256]{2,0,1:T(8,128)(2,1)S(1)}, u32[]{:S(2)}, u32[]{:S(2)}) async-start(bf16[32,32,256]{2,0,1:T(8,128)(2,1)} %copy.38), calls=%async_computation.1 | async-start | bytes 1048576 | tf_op jit(solution)/shard_map/all_to_all | solution.py:52
  38.0 15.3 %all-to-all-done.1 = bf16[32,32,256]{2,0,1:T(8,128)(2,1)S(1)} async-done(((bf16[32,32,256]{2,0,1:T(8,128)(2,1)}), bf16[32,32,256]{2,0,1:T(8,128)(2,1)S(1)}, u32[]{:S(2)}, u32[]{:S(2)}) %all-to-all-start.1) | async-done | bytes 524320 | tf_op jit(solution)/shard_map/all_to_all | solution.py:52
  53.2 3.9 %copy.39 = bf16[32,32,256]{1,0,2:T(8,128)(2,1)} copy(bf16[32,32,256]{2,0,1:T(8,128)(2,1)S(1)} %all-to-all-done.1) | data formatting | bytes 1048576 | tf_op jit(solution)/shard_map/all_to_all | solution.py:52
  57.2 2.2 convolution_bitcast_fusion.1
  60.5 1.8 fusion.25
  62.4 3.1 %collective-permute-start = (f32[1,4,32]{2,1,0:T(4,128)S(1)}, f32[1,4,32]{2,1,0:T(4,128)S(1)}, u32[]{:S(2)}, u32[]{:S(2)}) collective-permute-start(f32[1,4,32]{2,1,0:T(4,128)S(1)} %get-tuple-element.31), channel_id=1, source_target_pairs={{0,4},{4,8},{8,12},{12,16},{16,20},{20,24},{24,28},{1,5},{5,9},{9,... | collective-permute-start | bytes 1544 | tf_op jit(solution)/shard_map/ppermute | solution.py:17
  65.5 1.3 collective-permute-start.1
  67.5 3.5 %collective-permute-done.1 = f32[1,4,32]{2,1,0:T(4,128)S(1)} collective-permute-done((f32[1,4,32]{2,1,0:T(4,128)S(1)}, f32[1,4,32]{2,1,0:T(4,128)S(1)}, u32[]{:S(2)}, u32[]{:S(2)}) %collective-permute-start.1) | collective-permute-done | bytes 544 | tf_op jit(solution)/shard_map/ppermute | solution.py:20
  71.0 1.3 collective-permute-start.2
  72.3 1.3 collective-permute-start.3
  74.5 2.2 collective-permute-done.3
  78.6 40.8 %all-reduce.2 = (f32[]{:T(128)}, f32[]{:T(128)}) all-reduce(f32[]{:T(128)} %get-tuple-element.7, f32[]{:T(128)} %get-tuple-element.6), channel_id=1, replica_groups=mesh['gx'=8,'gy'=4] {'gx','gy'}, use_global_device_ids=true, to_apply=%region_1.0 | all-reduce | flops 2 | bytes 16 | tf_op jit(solution)/shard_map/psum | solution.py:75
  120.7 1.8 fusion.23
  122.5 4.4 %collective-permute-start.4 = (f32[1,4,32]{2,1,0:T(4,128)S(1)}, f32[1,4,32]{2,1,0:T(4,128)S(1)}, u32[]{:S(2)}, u32[]{:S(2)}) collective-permute-start(f32[1,4,32]{2,1,0:T(4,128)S(1)} %get-tuple-element.25), channel_id=1, source_target_pairs={{0,4},{4,8},{8,12},{12,16},{16,20},{20,24},{24,28},{1,5},{5,9},{9,... | collective-permute-start | bytes 1544 | tf_op jit(solution)/shard_map/ppermute | solution.py:17
  126.9 1.3 collective-permute-start.5
  128.2 4.2 %collective-permute-done.5 = f32[1,4,32]{2,1,0:T(4,128)S(1)} collective-permute-done((f32[1,4,32]{2,1,0:T(4,128)S(1)}, f32[1,4,32]{2,1,0:T(4,128)S(1)}, u32[]{:S(2)}, u32[]{:S(2)}) %collective-permute-start.5) | collective-permute-done | bytes 544 | tf_op jit(solution)/shard_map/ppermute | solution.py:20
  133.7 1.3 collective-permute-start.7
  135.9 1.4 collective-permute-done.7
  139.2 41.8 %all-reduce.1 = (f32[]{:T(128)}, f32[]{:T(128)}) all-reduce(f32[]{:T(128)} %get-tuple-element.5, f32[]{:T(128)} %get-tuple-element.4), channel_id=1, replica_groups=mesh['gx'=8,'gy'=4] {'gx','gy'}, use_global_device_ids=true, to_apply=%region_6.0 | all-reduce | flops 2 | bytes 16 | tf_op jit(solution)/shard_map/psum | solution.py:75
  185.7 1.8 fusion.21
  187.5 4.4 %collective-permute-start.8 = (f32[1,4,32]{2,1,0:T(4,128)S(1)}, f32[1,4,32]{2,1,0:T(4,128)S(1)}, u32[]{:S(2)}, u32[]{:S(2)}) collective-permute-start(f32[1,4,32]{2,1,0:T(4,128)S(1)} %get-tuple-element.23), channel_id=1, source_target_pairs={{0,4},{4,8},{8,12},{12,16},{16,20},{20,24},{24,28},{1,5},{5,9},{9,... | collective-permute-start | bytes 1544 | tf_op jit(solution)/shard_map/ppermute | solution.py:17
  192.0 1.3 collective-permute-start.9
  193.3 4.2 %collective-permute-done.9 = f32[1,4,32]{2,1,0:T(4,128)S(1)} collective-permute-done((f32[1,4,32]{2,1,0:T(4,128)S(1)}, f32[1,4,32]{2,1,0:T(4,128)S(1)}, u32[]{:S(2)}, u32[]{:S(2)}) %collective-permute-start.9) | collective-permute-done | bytes 544 | tf_op jit(solution)/shard_map/ppermute | solution.py:20
  198.8 1.3 collective-permute-start.11
  201.0 1.6 collective-permute-done.11
  204.5 41.9 %all-reduce = (f32[]{:T(128)}, f32[]{:T(128)}) all-reduce(f32[]{:T(128)} %get-tuple-element.3, f32[]{:T(128)} %get-tuple-element.2), channel_id=1, replica_groups=mesh['gx'=8,'gy'=4] {'gx','gy'}, use_global_device_ids=true, to_apply=%region_10.0 | all-reduce | flops 2 | bytes 16 | tf_op jit(solution)/shard_map/psum | solution.py:75
  (67 shorter events, 18.2 us)
Async XLA Ops:
  0.6 58.8 %copy-start = (f32[32,32,512]{2,1,0:T(8,128)S(1)}, f32[32,32,512]{2,1,0:T(8,128)}, u32[]{:S(2)}) copy-start(f32[32,32,512]{2,1,0:T(8,128)} %param.10) | copy-start | bytes 6291460
  2.8 8.0 %copy-start.4 = (pred[1024,8]{1,0:T(8,128)(4,1)}, pred[1024,8]{1,0:T(8,128)(4,1)S(1)}, u32[]{:S(2)}) copy-start(pred[1024,8]{1,0:T(8,128)(4,1)S(1)} %copy.34) | copy-start | bytes 24580
  4.9 15.4 %copy-start.3 = (bf16[32,8192]{1,0:T(8,128)(2,1)S(1)}, bf16[32,8192]{1,0:T(8,128)(2,1)}, u32[]{:S(2)}) copy-start(bf16[32,8192]{1,0:T(8,128)(2,1)} %param.6) | copy-start | bytes 1572868
  11.1 11.0 %copy-start.5 = (pred[1024,8]{1,0:T(8,128)(4,1)S(1)}, pred[1024,8]{1,0:T(8,128)(4,1)}, u32[]{:S(2)}) copy-start(pred[1024,8]{1,0:T(8,128)(4,1)} %copy-done.4) | copy-start | bytes 24580
  12.9 18.8 %all-to-all-start = ((bf16[32,2,128]{2,1,0:T(2,128)(2,1)}), bf16[32,2,128]{2,1,0:T(2,128)(2,1)S(1)}, u32[]{:S(2)}, u32[]{:S(2)}) async-start(bf16[32,2,128]{2,1,0:T(2,128)(2,1)} %reshape.100), calls=%async_computation | async-start | bytes 32768 | tf_op jit(solution)/shard_map/all_to_all | solution.py:53
  29.2 8.4 %copy-start.6 = (s32[32,4]{0,1:T(4,128)S(1)}, s32[32,4]{0,1:T(4,128)}, u32[]{:S(2)}) copy-start(s32[32,4]{0,1:T(4,128)} %param.9) | copy-start | bytes 1540
  31.8 21.5 %all-to-all-start.1 = ((bf16[32,32,256]{2,0,1:T(8,128)(2,1)}), bf16[32,32,256]{2,0,1:T(8,128)(2,1)S(1)}, u32[]{:S(2)}, u32[]{:S(2)}) async-start(bf16[32,32,256]{2,0,1:T(8,128)(2,1)} %copy.38), calls=%async_computation.1 | async-start | bytes 1048576 | tf_op jit(solution)/shard_map/all_to_all | solution.py:52
  59.4 7.4 %copy-start.1 = (bf16[32,32,256]{1,0,2:T(8,128)(2,1)S(1)}, bf16[32,32,256]{1,0,2:T(8,128)(2,1)}, u32[]{:S(2)}) copy-start(bf16[32,32,256]{1,0,2:T(8,128)(2,1)} %copy.39) | copy-start | bytes 1572868
  62.4 5.1 %collective-permute-start = (f32[1,4,32]{2,1,0:T(4,128)S(1)}, f32[1,4,32]{2,1,0:T(4,128)S(1)}, u32[]{:S(2)}, u32[]{:S(2)}) collective-permute-start(f32[1,4,32]{2,1,0:T(4,128)S(1)} %get-tuple-element.31), channel_id=1, source_target_pairs={{0,4},{4,8},{8,12},{12,16},{16,20},{20,24},{24,28},{1,5},{5,9},{9,... | collective-permute-start | bytes 1544 | tf_op jit(solution)/shard_map/ppermute | solution.py:17
  65.5 5.5 %collective-permute-start.1 = (f32[1,4,32]{2,1,0:T(4,128)S(1)}, f32[1,4,32]{2,1,0:T(4,128)S(1)}, u32[]{:S(2)}, u32[]{:S(2)}) collective-permute-start(f32[1,4,32]{2,1,0:T(4,128)S(1)} %get-tuple-element.32), channel_id=1, source_target_pairs={{4,0},{8,4},{12,8},{16,12},{20,16},{24,20},{28,24},{5,1},{9,5},{13... | collective-permute-start | bytes 1544 | tf_op jit(solution)/shard_map/ppermute | solution.py:20
  67.4 10.5 %copy-start.2 = (f32[32,512]{1,0:T(8,128)S(1)}, f32[32,512]{1,0:T(8,128)}, u32[]{:S(2)}) copy-start(f32[32,512]{1,0:T(8,128)} %param.11) | copy-start | bytes 196612
  71.0 3.5 %collective-permute-start.2 = (f32[10,1,32]{2,1,0:T(1,128)S(1)}, f32[10,1,32]{2,1,0:T(1,128)S(1)}, u32[]{:S(2)}, u32[]{:S(2)}) collective-permute-start(f32[10,1,32]{2,1,0:T(1,128)S(1)} %get-tuple-element.21), channel_id=1, source_target_pairs={{0,1},{1,2},{2,3},{4,5},{5,6},{6,7},{8,9},{9,10},{10,11},{12,13},{... | collective-permute-start | bytes 3848 | tf_op jit(solution)/shard_map/ppermute | solution.py:17
  72.3 4.4 %collective-permute-start.3 = (f32[10,1,32]{2,1,0:T(1,128)S(1)}, f32[10,1,32]{2,1,0:T(1,128)S(1)}, u32[]{:S(2)}, u32[]{:S(2)}) collective-permute-start(f32[10,1,32]{2,1,0:T(1,128)S(1)} %get-tuple-element.22), channel_id=1, source_target_pairs={{1,0},{2,1},{3,2},{5,4},{6,5},{7,6},{9,8},{10,9},{11,10},{13,12},{... | collective-permute-start | bytes 3848 | tf_op jit(solution)/shard_map/ppermute | solution.py:20
  122.5 5.7 %collective-permute-start.4 = (f32[1,4,32]{2,1,0:T(4,128)S(1)}, f32[1,4,32]{2,1,0:T(4,128)S(1)}, u32[]{:S(2)}, u32[]{:S(2)}) collective-permute-start(f32[1,4,32]{2,1,0:T(4,128)S(1)} %get-tuple-element.25), channel_id=1, source_target_pairs={{0,4},{4,8},{8,12},{12,16},{16,20},{20,24},{24,28},{1,5},{5,9},{9,... | collective-permute-start | bytes 1544 | tf_op jit(solution)/shard_map/ppermute | solution.py:17
  126.9 5.5 %collective-permute-start.5 = (f32[1,4,32]{2,1,0:T(4,128)S(1)}, f32[1,4,32]{2,1,0:T(4,128)S(1)}, u32[]{:S(2)}, u32[]{:S(2)}) collective-permute-start(f32[1,4,32]{2,1,0:T(4,128)S(1)} %get-tuple-element.26), channel_id=1, source_target_pairs={{4,0},{8,4},{12,8},{16,12},{20,16},{24,20},{28,24},{5,1},{9,5},{13... | collective-permute-start | bytes 1544 | tf_op jit(solution)/shard_map/ppermute | solution.py:20
  132.4 3.5 %collective-permute-start.6 = (f32[10,1,32]{2,1,0:T(1,128)S(1)}, f32[10,1,32]{2,1,0:T(1,128)S(1)}, u32[]{:S(2)}, u32[]{:S(2)}) collective-permute-start(f32[10,1,32]{2,1,0:T(1,128)S(1)} %get-tuple-element.19), channel_id=1, source_target_pairs={{0,1},{1,2},{2,3},{4,5},{5,6},{6,7},{8,9},{9,10},{10,11},{12,13},{... | collective-permute-start | bytes 3848 | tf_op jit(solution)/shard_map/ppermute | solution.py:17
  133.7 3.7 %collective-permute-start.7 = (f32[10,1,32]{2,1,0:T(1,128)S(1)}, f32[10,1,32]{2,1,0:T(1,128)S(1)}, u32[]{:S(2)}, u32[]{:S(2)}) collective-permute-start(f32[10,1,32]{2,1,0:T(1,128)S(1)} %get-tuple-element.20), channel_id=1, source_target_pairs={{1,0},{2,1},{3,2},{5,4},{6,5},{7,6},{9,8},{10,9},{11,10},{13,12},{... | collective-permute-start | bytes 3848 | tf_op jit(solution)/shard_map/ppermute | solution.py:20
  187.5 5.8 %collective-permute-start.8 = (f32[1,4,32]{2,1,0:T(4,128)S(1)}, f32[1,4,32]{2,1,0:T(4,128)S(1)}, u32[]{:S(2)}, u32[]{:S(2)}) collective-permute-start(f32[1,4,32]{2,1,0:T(4,128)S(1)} %get-tuple-element.23), channel_id=1, source_target_pairs={{0,4},{4,8},{8,12},{12,16},{16,20},{20,24},{24,28},{1,5},{5,9},{9,... | collective-permute-start | bytes 1544 | tf_op jit(solution)/shard_map/ppermute | solution.py:17
  192.0 5.5 %collective-permute-start.9 = (f32[1,4,32]{2,1,0:T(4,128)S(1)}, f32[1,4,32]{2,1,0:T(4,128)S(1)}, u32[]{:S(2)}, u32[]{:S(2)}) collective-permute-start(f32[1,4,32]{2,1,0:T(4,128)S(1)} %get-tuple-element.24), channel_id=1, source_target_pairs={{4,0},{8,4},{12,8},{16,12},{20,16},{24,20},{28,24},{5,1},{9,5},{13... | collective-permute-start | bytes 1544 | tf_op jit(solution)/shard_map/ppermute | solution.py:20
  197.5 3.5 %collective-permute-start.10 = (f32[10,1,32]{2,1,0:T(1,128)S(1)}, f32[10,1,32]{2,1,0:T(1,128)S(1)}, u32[]{:S(2)}, u32[]{:S(2)}) collective-permute-start(f32[10,1,32]{2,1,0:T(1,128)S(1)} %get-tuple-element.17), channel_id=1, source_target_pairs={{0,1},{1,2},{2,3},{4,5},{5,6},{6,7},{8,9},{9,10},{10,11},{12,13},{... | collective-permute-start | bytes 3848 | tf_op jit(solution)/shard_map/ppermute | solution.py:17
  198.8 3.8 %collective-permute-start.11 = (f32[10,1,32]{2,1,0:T(1,128)S(1)}, f32[10,1,32]{2,1,0:T(1,128)S(1)}, u32[]{:S(2)}, u32[]{:S(2)}) collective-permute-start(f32[10,1,32]{2,1,0:T(1,128)S(1)} %get-tuple-element.18), channel_id=1, source_target_pairs={{1,0},{2,1},{3,2},{5,4},{6,5},{7,6},{9,8},{10,9},{11,10},{13,12},{... | collective-permute-start | bytes 3848 | tf_op jit(solution)/shard_map/ppermute | solution.py:20
where the time goes:
time: 252 us; the launch traced here: 251 us
  blocking collectives  124 us (49%)
  starting transfers between devices  36.7 us (15%)
  waiting for transfers between devices  32.3 us (13%)
  matrix products  28.5 us (11%)
  local copies, waits for them, and re-layouts  12.6 us (5%)
  between operations  11.1 us (4%)
  other arithmetic  5.47 us (2%)
    psum x3, blocking collectives, two_products(): lax.psum((jnp.sum(values * values), jnp.sum(values * image)), ('gx', 'gy'))  124 us
    ppermute x6, waiting for transfers between devices, extended(): lax.ppermute(lax.slice_in_dim(block, 0, width, axis=dim), axis, backward)  17 us
    ppermute x6, starting transfers between devices, extended(): lax.ppermute(lax.slice_in_dim(block, block.shape[dim] - width, None, axis...  15.8 us
    all_to_all x1, waiting for transfers between devices, shards(): lax.all_to_all(sending, ('gx', 'gy'), split_axis=1, concat_axis=1, tiled=...  15.3 us
    ppermute x6, starting transfers between devices, extended(): lax.ppermute(lax.slice_in_dim(block, 0, width, axis=dim), axis, backward)  7.75 us
    all_to_all x1, starting transfers between devices, shards(): lax.all_to_all(target_rows, ('gx', 'gy'), split_axis=1, concat_axis=1, ti...  7.33 us
    dot_general x1, matrix products, shards(): jnp.einsum('ibd,bcd->ibc', blocks, choose, preferred_element_type=jnp.flo...  7.12 us
    dot_general x1, matrix products, shards(): jnp.einsum('bd,bcd->bc', target_blocks, choose, preferred_element_type=jn...  5.85 us
  transfers between devices with their start and end apart: 14, of which 7 were waited for; matrix products, arithmetic and copies ran while one was open for 6% of the time, Pallas kernels for 0%

commit v1 on v0

--- a/solution.py
+++ b/solution.py
@@ -48,8 +48,20 @@
     ).astype(jnp.bfloat16)
     sending = picked.reshape(feat_count, devices, local_bricks * slots)
     target_rows = targets.reshape(1, devices, local_bricks * slots)
+
+    def name_quarters(field_in):
+        return jnp.concatenate(
+            lax.all_to_all(
+                jnp.stack(jnp.split(field_in, lax.axis_size(("gx", "gy")), axis=1)),
+                axis_name=("gx", "gy"),
+                split_axis=0,
+                concat_axis=0,
+            ),
+            axis=1,
+        )
+
     got_feats, got_targets = (
-        lax.all_to_all(sending, ("gx", "gy"), split_axis=1, concat_axis=1, tiled=True),
+        name_quarters(sending),
         lax.all_to_all(target_rows, ("gx", "gy"), split_axis=1, concat_axis=1, tiled=True),
     )
     got_feats = got_feats.reshape(feat_count, devices, local_bricks, slots)

time: 252 us -> 296 us (1.17)
  local copies, waits for them, and re-layouts: 12.6 us -> 55.8 us
    unnamed x18 -> x81, local copies, waits for them, and re-layouts: 2.95 us -> 47.2 us
    all_to_all x1 -> x0, local copies, waits for them, and re-layouts: 3.94 us -> none  [shards(): lax.all_to_all(sending, ('gx', 'gy'), split_axis=1, concat_axis=1, tiled=...]
  transfers between devices with their start and end apart: 14 -> 14, of which waited for: 7 -> 7; matrix products, arithmetic and copies ran while one was open for 6% -> 20% of each run, Pallas kernels for 0% -> 0%
where the time goes in v1:
time: 296 us; the launch traced here: 293 us
  blocking collectives  124 us (42%)
  local copies, waits for them, and re-layouts  55.8 us (19%)
  starting transfers between devices  36.9 us (12%)
  waiting for transfers between devices  32.1 us (11%)
  matrix products  27.5 us (9%)
  between operations  11.1 us (4%)
  other arithmetic  5.54 us (2%)
    psum x3, blocking collectives, two_products(): lax.psum((jnp.sum(values * values), jnp.sum(values * image)), ('gx', 'gy'))  124 us
    unnamed x81, local copies, waits for them, and re-layouts  47.2 us
    ppermute x6, waiting for transfers between devices, extended(): lax.ppermute(lax.slice_in_dim(block, 0, width, axis=dim), axis, backward)  16.9 us
    ppermute x6, starting transfers between devices, extended(): lax.ppermute(lax.slice_in_dim(block, block.shape[dim] - width, None, axis...  15.8 us
    all_to_all x1, waiting for transfers between devices, name_quarters(): lax.all_to_all(jnp.stack(jnp.split(field_in, lax.axis_size(('gx', 'gy')),...  15.3 us
    ppermute x6, starting transfers between devices, extended(): lax.ppermute(lax.slice_in_dim(block, 0, width, axis=dim), axis, backward)  7.93 us
    all_to_all x1, starting transfers between devices, shards(): lax.all_to_all(target_rows, ('gx', 'gy'), split_axis=1, concat_axis=1, ti...  7.33 us
    dot_general x1, matrix products, shards(): jnp.einsum('ibd,bcd->ibc', blocks, choose, preferred_element_type=jnp.flo...  6.12 us
  transfers between devices with their start and end apart: 14, of which 7 were waited for; matrix products, arithmetic and copies ran while one was open for 20% of the time, Pallas kernels for 0%

profile of v1, /device:TPU:0, one launch (start us, length us, event | category | flops | bytes accessed | tf_op | source)
XLA Modules:
  0.0 293.4 jit_solution(17849293042728505420)
XLA Ops:
  2.8 2.1 reshape.98
  4.9 5.8 %fusion.3 = f32[1024,1,8]{2,1,0:T(1,128)S(1)} fusion(bf16[1024,8,1]{1,2,0:T(2,128)(2,1)} %reshape.98, s32[1024,8]{1,0:T(8,128)S(1)} %copy.33, pred[1024,8]{1,0:T(8,128)(4,1)S(1)} %copy.34), kind=kOutput, calls=%fused_computation.3 | convolution fusion | flops 262144 | bytes 90112 | tf_op jit(solution)/shard_map/bd,bcd->bc/dot_general | solution.py:46
  12.9 7.3 %all-to-all-start = ((bf16[32,2,128]{2,1,0:T(2,128)(2,1)}), bf16[32,2,128]{2,1,0:T(2,128)(2,1)S(1)}, u32[]{:S(2)}, u32[]{:S(2)}) async-start(bf16[32,2,128]{2,1,0:T(2,128)(2,1)} %reshape.100), calls=%async_computation | async-start | bytes 32768 | tf_op jit(solution)/shard_map/all_to_all | solution.py:65
  20.3 1.8 copy.37
  22.1 6.1 %fusion.10 = bf16[1024,8,32]{2,1,0:T(8,128)(2,1)S(1)} fusion(bf16[32,8192]{0,1:T(8,128)(2,1)} %copy.37, s32[1024,8]{1,0:T(8,128)S(1)} %copy.33, pred[1024,8]{1,0:T(8,128)(4,1)S(1)} %copy-done.5), kind=kOutput, calls=%fused_computation.9 | convolution fusion | flops 4587520 | bytes 1089536 | tf_op jit(solution)/shard_map/ibd,bcd->ibc/dot_general | solution.py:42
  29.2 1.5 copy.108
  32.0 1.5 copy.109
  33.5 1.5 copy.110
  35.0 1.5 copy.111
  36.5 1.5 copy.112
  38.1 1.5 copy.113
  39.6 1.5 copy.114
  41.1 1.5 copy.115
  44.1 1.5 copy.117
  74.0 5.8 %all-to-all-start.1 = ((bf16[32,32,1,256]{3,1,2,0:T(8,128)(2,1)}), bf16[32,32,1,256]{3,1,2,0:T(8,128)(2,1)S(1)}, u32[]{:S(2)}, u32[]{:S(2)}) async-start(bf16[32,32,1,256]{3,1,2,0:T(8,128)(2,1)} %constant_dynamic-update-slice_fusion), calls=%async_computation.1 | async-start | bytes 1048576 | tf_op jit(solution)/shard_map/all_to_all | solution.py:54
  80.2 15.3 %all-to-all-done.1 = bf16[32,32,1,256]{3,1,2,0:T(8,128)(2,1)S(1)} async-done(((bf16[32,32,1,256]{3,1,2,0:T(8,128)(2,1)}), bf16[32,32,1,256]{3,1,2,0:T(8,128)(2,1)S(1)}, u32[]{:S(2)}, u32[]{:S(2)}) %all-to-all-start.1) | async-done | bytes 524320 | tf_op jit(solution)/shard_map/all_to_all | solution.py:54
  95.5 4.0 %copy.70 = bf16[32,32,1,256]{1,0,3,2:T(8,128)(2,1)} copy(bf16[32,32,1,256]{3,0,2,1:T(8,128)(2,1)S(1)} %bitcast.223) | data formatting | bytes 1048576 | tf_op jit(solution)/shard_map/reshape | solution.py:53
  99.4 2.2 convolution_bitcast_fusion.1
  102.8 1.8 fusion.25
  104.6 3.1 %collective-permute-start = (f32[1,4,32]{2,1,0:T(4,128)S(1)}, f32[1,4,32]{2,1,0:T(4,128)S(1)}, u32[]{:S(2)}, u32[]{:S(2)}) collective-permute-start(f32[1,4,32]{2,1,0:T(4,128)S(1)} %get-tuple-element.63), channel_id=1, source_target_pairs={{0,4},{4,8},{8,12},{12,16},{16,20},{20,24},{24,28},{1,5},{5,9},{9,... | collective-permute-start | bytes 1544 | tf_op jit(solution)/shard_map/ppermute | solution.py:17
  109.7 3.5 %collective-permute-done.1 = f32[1,4,32]{2,1,0:T(4,128)S(1)} collective-permute-done((f32[1,4,32]{2,1,0:T(4,128)S(1)}, f32[1,4,32]{2,1,0:T(4,128)S(1)}, u32[]{:S(2)}, u32[]{:S(2)}) %collective-permute-start.1) | collective-permute-done | bytes 544 | tf_op jit(solution)/shard_map/ppermute | solution.py:20
  116.9 2.0 collective-permute-done.3
  120.8 40.6 %all-reduce.2 = (f32[]{:T(128)}, f32[]{:T(128)}) all-reduce(f32[]{:T(128)} %get-tuple-element.7, f32[]{:T(128)} %get-tuple-element.6), channel_id=1, replica_groups=mesh['gx'=8,'gy'=4] {'gx','gy'}, use_global_device_ids=true, to_apply=%region_1.0 | all-reduce | flops 2 | bytes 16 | tf_op jit(solution)/shard_map/psum | solution.py:87
  162.8 1.8 fusion.23
  164.6 4.4 %collective-permute-start.4 = (f32[1,4,32]{2,1,0:T(4,128)S(1)}, f32[1,4,32]{2,1,0:T(4,128)S(1)}, u32[]{:S(2)}, u32[]{:S(2)}) collective-permute-start(f32[1,4,32]{2,1,0:T(4,128)S(1)} %get-tuple-element.57), channel_id=1, source_target_pairs={{0,4},{4,8},{8,12},{12,16},{16,20},{20,24},{24,28},{1,5},{5,9},{9,... | collective-permute-start | bytes 1544 | tf_op jit(solution)/shard_map/ppermute | solution.py:17
  170.3 4.2 %collective-permute-done.5 = f32[1,4,32]{2,1,0:T(4,128)S(1)} collective-permute-done((f32[1,4,32]{2,1,0:T(4,128)S(1)}, f32[1,4,32]{2,1,0:T(4,128)S(1)}, u32[]{:S(2)}, u32[]{:S(2)}) %collective-permute-start.5) | collective-permute-done | bytes 544 | tf_op jit(solution)/shard_map/ppermute | solution.py:20
  181.4 41.9 %all-reduce.1 = (f32[]{:T(128)}, f32[]{:T(128)}) all-reduce(f32[]{:T(128)} %get-tuple-element.5, f32[]{:T(128)} %get-tuple-element.4), channel_id=1, replica_groups=mesh['gx'=8,'gy'=4] {'gx','gy'}, use_global_device_ids=true, to_apply=%region_6.0 | all-reduce | flops 2 | bytes 16 | tf_op jit(solution)/shard_map/psum | solution.py:87
  228.0 1.8 fusion.21
  229.8 4.4 %collective-permute-start.8 = (f32[1,4,32]{2,1,0:T(4,128)S(1)}, f32[1,4,32]{2,1,0:T(4,128)S(1)}, u32[]{:S(2)}, u32[]{:S(2)}) collective-permute-start(f32[1,4,32]{2,1,0:T(4,128)S(1)} %get-tuple-element.55), channel_id=1, source_target_pairs={{0,4},{4,8},{8,12},{12,16},{16,20},{20,24},{24,28},{1,5},{5,9},{9,... | collective-permute-start | bytes 1544 | tf_op jit(solution)/shard_map/ppermute | solution.py:17
  235.5 4.2 %collective-permute-done.9 = f32[1,4,32]{2,1,0:T(4,128)S(1)} collective-permute-done((f32[1,4,32]{2,1,0:T(4,128)S(1)}, f32[1,4,32]{2,1,0:T(4,128)S(1)}, u32[]{:S(2)}, u32[]{:S(2)}) %collective-permute-start.9) | collective-permute-done | bytes 544 | tf_op jit(solution)/shard_map/ppermute | solution.py:20
  243.2 1.6 collective-permute-done.11
  246.7 41.9 %all-reduce = (f32[]{:T(128)}, f32[]{:T(128)}) all-reduce(f32[]{:T(128)} %get-tuple-element.3, f32[]{:T(128)} %get-tuple-element.2), channel_id=1, replica_groups=mesh['gx'=8,'gy'=4] {'gx','gy'}, use_global_device_ids=true, to_apply=%region_10.0 | all-reduce | flops 2 | bytes 16 | tf_op jit(solution)/shard_map/psum | solution.py:87
  (132 shorter events, 61.0 us)
Async XLA Ops:
  0.6 101.0 %copy-start = (f32[32,32,512]{2,1,0:T(8,128)S(1)}, f32[32,32,512]{2,1,0:T(8,128)}, u32[]{:S(2)}) copy-start(f32[32,32,512]{2,1,0:T(8,128)} %param.10) | copy-start | bytes 6291460
  2.8 8.0 %copy-start.4 = (pred[1024,8]{1,0:T(8,128)(4,1)}, pred[1024,8]{1,0:T(8,128)(4,1)S(1)}, u32[]{:S(2)}) copy-start(pred[1024,8]{1,0:T(8,128)(4,1)S(1)} %copy.34) | copy-start | bytes 24580
  4.9 15.4 %copy-start.3 = (bf16[32,8192]{1,0:T(8,128)(2,1)S(1)}, bf16[32,8192]{1,0:T(8,128)(2,1)}, u32[]{:S(2)}) copy-start(bf16[32,8192]{1,0:T(8,128)(2,1)} %param.6) | copy-start | bytes 1572868
  11.1 11.0 %copy-start.5 = (pred[1024,8]{1,0:T(8,128)(4,1)S(1)}, pred[1024,8]{1,0:T(8,128)(4,1)}, u32[]{:S(2)}) copy-start(pred[1024,8]{1,0:T(8,128)(4,1)} %copy-done.4) | copy-start | bytes 24580
  12.9 61.1 %all-to-all-start = ((bf16[32,2,128]{2,1,0:T(2,128)(2,1)}), bf16[32,2,128]{2,1,0:T(2,128)(2,1)S(1)}, u32[]{:S(2)}, u32[]{:S(2)}) async-start(bf16[32,2,128]{2,1,0:T(2,128)(2,1)} %reshape.100), calls=%async_computation | async-start | bytes 32768 | tf_op jit(solution)/shard_map/all_to_all | solution.py:65
  46.3 33.5 %copy-start.6 = (s32[32,4]{0,1:T(4,128)S(1)}, s32[32,4]{0,1:T(4,128)}, u32[]{:S(2)}) copy-start(s32[32,4]{0,1:T(4,128)} %param.9) | copy-start | bytes 1540
  74.0 21.5 %all-to-all-start.1 = ((bf16[32,32,1,256]{3,1,2,0:T(8,128)(2,1)}), bf16[32,32,1,256]{3,1,2,0:T(8,128)(2,1)S(1)}, u32[]{:S(2)}, u32[]{:S(2)}) async-start(bf16[32,32,1,256]{3,1,2,0:T(8,128)(2,1)} %constant_dynamic-update-slice_fusion), calls=%async_computation.1 | async-start | bytes 1048576 | tf_op jit(solution)/shard_map/all_to_all | solution.py:54
  101.6 7.4 %copy-start.1 = (bf16[32,32,1,256]{1,0,3,2:T(8,128)(2,1)S(1)}, bf16[32,32,1,256]{1,0,3,2:T(8,128)(2,1)}, u32[]{:S(2)}) copy-start(bf16[32,32,1,256]{1,0,3,2:T(8,128)(2,1)} %copy.70) | copy-start | bytes 1572868
  104.6 5.1 %collective-permute-start = (f32[1,4,32]{2,1,0:T(4,128)S(1)}, f32[1,4,32]{2,1,0:T(4,128)S(1)}, u32[]{:S(2)}, u32[]{:S(2)}) collective-permute-start(f32[1,4,32]{2,1,0:T(4,128)S(1)} %get-tuple-element.63), channel_id=1, source_target_pairs={{0,4},{4,8},{8,12},{12,16},{16,20},{20,24},{24,28},{1,5},{5,9},{9,... | collective-permute-start | bytes 1544 | tf_op jit(solution)/shard_map/ppermute | solution.py:17
  107.7 5.5 %collective-permute-start.1 = (f32[1,4,32]{2,1,0:T(4,128)S(1)}, f32[1,4,32]{2,1,0:T(4,128)S(1)}, u32[]{:S(2)}, u32[]{:S(2)}) collective-permute-start(f32[1,4,32]{2,1,0:T(4,128)S(1)} %get-tuple-element.64), channel_id=1, source_target_pairs={{4,0},{8,4},{12,8},{16,12},{20,16},{24,20},{28,24},{5,1},{9,5},{13... | collective-permute-start | bytes 1544 | tf_op jit(solution)/shard_map/ppermute | solution.py:20
  109.7 10.5 %copy-start.2 = (f32[32,512]{1,0:T(8,128)S(1)}, f32[32,512]{1,0:T(8,128)}, u32[]{:S(2)}) copy-start(f32[32,512]{1,0:T(8,128)} %param.11) | copy-start | bytes 196612
  113.2 3.7 %collective-permute-start.2 = (f32[10,1,32]{2,1,0:T(1,128)S(1)}, f32[10,1,32]{2,1,0:T(1,128)S(1)}, u32[]{:S(2)}, u32[]{:S(2)}) collective-permute-start(f32[10,1,32]{2,1,0:T(1,128)S(1)} %get-tuple-element.53), channel_id=1, source_target_pairs={{0,1},{1,2},{2,3},{4,5},{5,6},{6,7},{8,9},{9,10},{10,11},{12,13},{... | collective-permute-start | bytes 3848 | tf_op jit(solution)/shard_map/ppermute | solution.py:17
  114.5 4.4 %collective-permute-start.3 = (f32[10,1,32]{2,1,0:T(1,128)S(1)}, f32[10,1,32]{2,1,0:T(1,128)S(1)}, u32[]{:S(2)}, u32[]{:S(2)}) collective-permute-start(f32[10,1,32]{2,1,0:T(1,128)S(1)} %get-tuple-element.54), channel_id=1, source_target_pairs={{1,0},{2,1},{3,2},{5,4},{6,5},{7,6},{9,8},{10,9},{11,10},{13,12},{... | collective-permute-start | bytes 3848 | tf_op jit(solution)/shard_map/ppermute | solution.py:20
  164.6 5.7 %collective-permute-start.4 = (f32[1,4,32]{2,1,0:T(4,128)S(1)}, f32[1,4,32]{2,1,0:T(4,128)S(1)}, u32[]{:S(2)}, u32[]{:S(2)}) collective-permute-start(f32[1,4,32]{2,1,0:T(4,128)S(1)} %get-tuple-element.57), channel_id=1, source_target_pairs={{0,4},{4,8},{8,12},{12,16},{16,20},{20,24},{24,28},{1,5},{5,9},{9,... | collective-permute-start | bytes 1544 | tf_op jit(solution)/shard_map/ppermute | solution.py:17
  169.0 5.5 %collective-permute-start.5 = (f32[1,4,32]{2,1,0:T(4,128)S(1)}, f32[1,4,32]{2,1,0:T(4,128)S(1)}, u32[]{:S(2)}, u32[]{:S(2)}) collective-permute-start(f32[1,4,32]{2,1,0:T(4,128)S(1)} %get-tuple-element.58), channel_id=1, source_target_pairs={{4,0},{8,4},{12,8},{16,12},{20,16},{24,20},{28,24},{5,1},{9,5},{13... | collective-permute-start | bytes 1544 | tf_op jit(solution)/shard_map/ppermute | solution.py:20
  174.5 3.5 %collective-permute-start.6 = (f32[10,1,32]{2,1,0:T(1,128)S(1)}, f32[10,1,32]{2,1,0:T(1,128)S(1)}, u32[]{:S(2)}, u32[]{:S(2)}) collective-permute-start(f32[10,1,32]{2,1,0:T(1,128)S(1)} %get-tuple-element.51), channel_id=1, source_target_pairs={{0,1},{1,2},{2,3},{4,5},{5,6},{6,7},{8,9},{9,10},{10,11},{12,13},{... | collective-permute-start | bytes 3848 | tf_op jit(solution)/shard_map/ppermute | solution.py:17
  175.8 3.7 %collective-permute-start.7 = (f32[10,1,32]{2,1,0:T(1,128)S(1)}, f32[10,1,32]{2,1,0:T(1,128)S(1)}, u32[]{:S(2)}, u32[]{:S(2)}) collective-permute-start(f32[10,1,32]{2,1,0:T(1,128)S(1)} %get-tuple-element.52), channel_id=1, source_target_pairs={{1,0},{2,1},{3,2},{5,4},{6,5},{7,6},{9,8},{10,9},{11,10},{13,12},{... | collective-permute-start | bytes 3848 | tf_op jit(solution)/shard_map/ppermute | solution.py:20
  229.8 5.7 %collective-permute-start.8 = (f32[1,4,32]{2,1,0:T(4,128)S(1)}, f32[1,4,32]{2,1,0:T(4,128)S(1)}, u32[]{:S(2)}, u32[]{:S(2)}) collective-permute-start(f32[1,4,32]{2,1,0:T(4,128)S(1)} %get-tuple-element.55), channel_id=1, source_target_pairs={{0,4},{4,8},{8,12},{12,16},{16,20},{20,24},{24,28},{1,5},{5,9},{9,... | collective-permute-start | bytes 1544 | tf_op jit(solution)/shard_map/ppermute | solution.py:17
  234.2 5.5 %collective-permute-start.9 = (f32[1,4,32]{2,1,0:T(4,128)S(1)}, f32[1,4,32]{2,1,0:T(4,128)S(1)}, u32[]{:S(2)}, u32[]{:S(2)}) collective-permute-start(f32[1,4,32]{2,1,0:T(4,128)S(1)} %get-tuple-element.56), channel_id=1, source_target_pairs={{4,0},{8,4},{12,8},{16,12},{20,16},{24,20},{28,24},{5,1},{9,5},{13... | collective-permute-start | bytes 1544 | tf_op jit(solution)/shard_map/ppermute | solution.py:20
  239.7 3.5 %collective-permute-start.10 = (f32[10,1,32]{2,1,0:T(1,128)S(1)}, f32[10,1,32]{2,1,0:T(1,128)S(1)}, u32[]{:S(2)}, u32[]{:S(2)}) collective-permute-start(f32[10,1,32]{2,1,0:T(1,128)S(1)} %get-tuple-element.49), channel_id=1, source_target_pairs={{0,1},{1,2},{2,3},{4,5},{5,6},{6,7},{8,9},{9,10},{10,11},{12,13},{... | collective-permute-start | bytes 3848 | tf_op jit(solution)/shard_map/ppermute | solution.py:17
  241.0 3.8 %collective-permute-start.11 = (f32[10,1,32]{2,1,0:T(1,128)S(1)}, f32[10,1,32]{2,1,0:T(1,128)S(1)}, u32[]{:S(2)}, u32[]{:S(2)}) collective-permute-start(f32[10,1,32]{2,1,0:T(1,128)S(1)} %get-tuple-element.50), channel_id=1, source_target_pairs={{1,0},{2,1},{3,2},{5,4},{6,5},{7,6},{9,8},{10,9},{11,10},{13,12},{... | collective-permute-start | bytes 3848 | tf_op jit(solution)/shard_map/ppermute | solution.py:20
